TPU v7x, 32 devices: a whole 2x2x4 slice. The times are simulated.
32 devices in a mesh: dp: 2 (over y), ctx: 4 (over x, core), tensor: 4 (over z).
Axes of the slice: x: 2, y: 2, z: 4, core: 2. Of those that a mesh axis runs over, the one named last changes fastest.
Arguments:
- residual: bfloat16 [2048, 3584], P(('dp', 'ctx', 'tensor')), parts along dimension 0, may hold values from -6 to 6
- queries: bfloat16 [2048, 1024], P(('dp', 'ctx'), 'tensor'), parts along dimension 0, may hold values from -8 to 8
- key_heads: bfloat16 [2048, 512], P(('dp', 'ctx'), 'tensor'), parts along dimension 0, may hold values from -8 to 8
- value_heads: bfloat16 [2048, 512], P(('dp', 'ctx'), 'tensor'), parts along dimension 0, may hold values from -6 to 6
- doc_blocks: int32 [12], P('dp'), parts along dimension 0, may hold values from 1 to 16, 32 in all
- out_weight: bfloat16 [1024, 3584], P('tensor'), may hold values from -0.53125 to 0.53125
- post_gain: float32 [3584], replicated, may hold values from 0.1 to 1.9
- ffn_gain: float32 [3584], replicated, may hold values from 0.1 to 1.9
- gate_weight: bfloat16 [3584, 3584], P('ctx', 'tensor'), may hold values from -0.09375 to 0.09375
- up_weight: bfloat16 [3584, 3584], P('ctx', 'tensor'), may hold values from -0.09375 to 0.09375
Outputs:
- mixed_stream: bfloat16 [2048, 3584], P(('dp', 'ctx', 'tensor')), parts along dimension 0
- ffn_hidden: bfloat16 [2048, 3584], P(('dp', 'ctx'), 'tensor'), parts along dimension 0
There are 2 independent parts, one for each index of `dp`. A program takes and returns all parts, laid end to end along the dimension named above; an argument that names none is the same for every part. Nothing has to cross between parts.
Inputs may be any that keep to these rules, and one draw needn't show every extreme that they name: `doc_blocks`: the lengths, in blocks of 32 positions, of the 6 documents packed in order into the sequence; they sum to 32, and the longest has exactly 16 blocks.
All inputs are finite; a program needn't handle non-finite values.
Results may differ from a plain program's by a relative error of at most 0.025.
Values may be sent and summed in bfloat16 or wider, within the bound.
A program may use at most 64 MiB of HBM per device.

v0:
```python
import jax
import jax.numpy as jnp
from jax import lax
from jax.sharding import PartitionSpec as P

BLOCK = 32
SOFT_CAP = 50.0
NORM_EPS = 1e-06
ROPE_BASE = 10000.0


def partner_2(value, axis, apart):
    mask = 2**apart
    pairs = [(source, source ^ mask) for source in range(lax.axis_size(axis))]
    return lax.ppermute(value, axis, pairs)


def rope_angles(positions, head_size):
    halfway = head_size // 2
    frequency = ROPE_BASE ** (-(jnp.arange(halfway, dtype=jnp.float32) * 2.0) / head_size)
    angles = positions.astype(jnp.float32)[:, None] * frequency[None, :]
    return (jnp.cos(angles), jnp.sin(angles))


def rotate(heads_in, cosine, sine_value, head_size):
    rows_here = heads_in.shape[0]
    reshaped = heads_in.astype(jnp.float32).reshape(rows_here, -1, head_size)
    leading = reshaped[:, :, : head_size // 2]
    trailing = reshaped[:, :, head_size // 2 :]
    cos_wide = cosine[:, None, :]
    sin_wide = sine_value[:, None, :]
    turned = jnp.concatenate(
        [leading * cos_wide - trailing * sin_wide, trailing * cos_wide + leading * sin_wide], axis=2
    )
    return turned.reshape(rows_here, -1).astype(jnp.bfloat16)


def doc_of(positions, doc_blocks):
    doc_ends = jnp.cumsum(doc_blocks)
    passed = positions[:, None] // BLOCK >= doc_ends[None, :]
    return jnp.sum(passed.astype(jnp.int32), axis=1)


def rms_scale(values):
    return values * lax.rsqrt(jnp.mean(values * values, axis=-1, keepdims=True) + NORM_EPS)


def gelu_gate(gate_sum, up_sum):
    return (jax.nn.gelu(gate_sum, approximate=True) * up_sum).astype(jnp.bfloat16)


def attend(query_rows, query_pos, query_doc, key_rows, value_rows, key_pos, key_doc, score_scale):
    scores = (
        lax.dot_general(
            query_rows, key_rows, (((1,), (1,)), ((), ())), preferred_element_type=jnp.float32
        )
        * score_scale
    )
    capped = SOFT_CAP * jnp.tanh(scores / SOFT_CAP)
    visible = (key_pos[None, :] <= query_pos[:, None]) & (key_doc[None, :] == query_doc[:, None])
    weights = jnp.where(visible, jnp.exp(capped), 0.0).astype(jnp.bfloat16)
    numerator = jnp.dot(weights, value_rows, preferred_element_type=jnp.float32)
    denominator = jnp.sum(weights.astype(jnp.float32), axis=1)
    return (numerator, denominator)


def join_halves(own_part, other_part, own_first):
    return jnp.where(
        own_first,
        jnp.concatenate([own_part, other_part], axis=2),
        jnp.concatenate([other_part, own_part], axis=2),
    )


def per_device(
    residual,
    queries,
    key_heads,
    value_heads,
    doc_blocks,
    out_weight,
    post_gain,
    ffn_gain,
    gate_weight,
    up_weight,
):
    tok_rows = queries.shape[0]
    head_size = queries.shape[1]
    score_scale = head_size ** (-0.5)
    query_pos = lax.axis_index("ctx") * tok_rows + jnp.arange(tok_rows, dtype=jnp.int32)
    query_doc = doc_of(query_pos, doc_blocks)
    cosine, sine_value = rope_angles(query_pos, head_size)
    query_rot = rotate(queries, cosine, sine_value, head_size)
    stacked = jnp.stack([key_heads, value_heads])
    own_first = lax.axis_index("tensor") % 2 == 0
    partner = partner_2(stacked, "tensor", 0)
    joined = join_halves(stacked, partner, own_first)
    key_rot = rotate(joined[0], cosine, sine_value, head_size)
    shard_pair = (
        lax.all_gather(key_rot, "ctx", axis=0, tiled=True),
        lax.all_gather(joined[1], "ctx", axis=0, tiled=True),
    )
    key_pos = jnp.arange(shard_pair[0].shape[0], dtype=jnp.int32)
    numerator, denominator = attend(
        query_rot,
        query_pos,
        query_doc,
        shard_pair[0],
        shard_pair[1],
        key_pos,
        doc_of(key_pos, doc_blocks),
        score_scale,
    )
    attended = (numerator / denominator[:, None]).astype(jnp.bfloat16)
    attn_rows = lax.psum_scatter(
        jnp.dot(attended, out_weight, preferred_element_type=jnp.float32).astype(jnp.bfloat16),
        "tensor",
        scatter_dimension=0,
        tiled=True,
    ).astype(jnp.float32)
    mixed_stream = (residual.astype(jnp.float32) + rms_scale(attn_rows) * post_gain).astype(
        jnp.bfloat16
    )
    ffn_input = (rms_scale(mixed_stream.astype(jnp.float32)) * ffn_gain).astype(jnp.bfloat16)
    gathered_rows = lax.all_gather(ffn_input, "tensor", axis=0, tiled=True)
    shard_pair = (
        lax.all_gather(gate_weight, "ctx", axis=0, tiled=True),
        lax.all_gather(up_weight, "ctx", axis=0, tiled=True),
    )
    gate_part = jnp.dot(gathered_rows, shard_pair[0], preferred_element_type=jnp.float32)
    up_part = jnp.dot(gathered_rows, shard_pair[1], preferred_element_type=jnp.float32)
    ffn_hidden = gelu_gate(gate_part, up_part)
    return (mixed_stream, ffn_hidden)


def solution(mesh):
    in_specs = (
        P(("dp", "ctx", "tensor"), None),
        P(("dp", "ctx"), "tensor"),
        P(("dp", "ctx"), "tensor"),
        P(("dp", "ctx"), "tensor"),
        P("dp"),
        P("tensor", None),
        P(),
        P(),
        P("ctx", "tensor"),
        P("ctx", "tensor"),
    )
    out_specs = (P(("dp", "ctx", "tensor"), None), P(("dp", "ctx"), "tensor"))
    return jax.shard_map(
        per_device, mesh=mesh, in_specs=in_specs, out_specs=out_specs, check_vma=False
    )
```

profile of v0, /device:TPU:0, one launch (start us, length us, event | category | flops | bytes accessed | tf_op | source)
XLA Modules:
  0.0 227.5 jit_solution(10332107046243191215)
XLA Ops:
  7.2 0.0 copy-start
  7.2 0.0 reduce-scatter.2.cloned.1.call-start
  7.2 1.0 pad_maximum_fusion
  8.2 3.1 %collective-permute-start = (bf16[2,256,128]{2,1,0:T(8,128)(2,1)S(1)}, bf16[2,256,128]{2,1,0:T(8,128)(2,1)S(1)}, u32[]{:S(2)}, u32[]{:S(2)}) collective-permute-start(bf16[2,256,128]{2,1,0:T(8,128)(2,1)S(1)} %pad_maximum_fusion), channel_id=1, source_target_pairs={{0,1},{1,0},{2,3},{3,2},{4,5},{5,4},{6,7},{7,6},{8,9},{9,8},{10,11... | collective-permute-start | bytes 393224 | tf_op jit(solution)/shard_map/ppermute | solution.py:15
  11.4 0.9 bitcast_convert_fusion
  12.3 0.8 reduce-window.8
  13.1 0.1 convert_reduce_fusion.2
  13.2 0.1 convert_reduce_fusion.1
  13.3 1.5 collective-permute-done
  14.9 1.0 maximum_select_fusion
  15.9 0.6 fusion.34
  16.5 7.3 %all-gather = bf16[1024,1,256]{2,0,1:T(8,128)(2,1)S(1)} all-gather(bf16[256,1,256]{2,0,1:T(8,128)(2,1)S(1)} %pad_maximum_fusion.1), channel_id=2, replica_groups=mesh['dp'=2,'ctx'=4,'tensor'=4] {'ctx'}, dimensions={0}, use_global_device_ids=true | all-gather | bytes 655360 | tf_op jit(solution)/shard_map/all_gather | solution.py:100
  23.9 7.3 %all-gather.1 = bf16[1,1024,256]{2,1,0:T(8,128)(2,1)S(1)} all-gather(bf16[1,256,256]{2,1,0:T(8,128)(2,1)S(1)} %get-tuple-element.8), channel_id=3, replica_groups=mesh['dp'=2,'ctx'=4,'tensor'=4] {'ctx'}, dimensions={1}, use_global_device_ids=true | all-gather | bytes 655360 | tf_op jit(solution)/shard_map/all_gather | solution.py:101
  31.1 0.7 convert_reduce_fusion
  31.8 0.0 copy-done
  31.8 2.4 %convolution_convert_fusion = bf16[256,3584]{1,0:T(8,128)(2,1)} fusion(bf16[256,3584]{1,0:T(8,128)(2,1)S(1)} %copy-done, bf16[256,1024]{1,0:T(8,128)(2,1)S(1)} %get-tuple-element.13, bf16[1,1024,256]{2,1,0:T(8,128)(2,1)S(1)} %all-gather.1, f32[256]{0:T(256)S(1)} %get-tuple-element.12), kind=kOutput, calls=%fused_computation | convolution fusion | flops 605028352 | bytes 4719616 | tf_op jit(solution)/shard_map/dot_general | solution.py:116
  34.2 0.0 copy-start.2
  34.2 0.0 copy-start.3
  34.2 0.0 copy-start.4
  34.2 0.0 reduce-scatter.2.cloned.1.call-update
  34.2 0.0 all-gather.6.cloned.1.call-start
  34.3 40.2 %reduce-scatter.2.cloned.1.call-done = bf16[64,3584]{1,0:T(8,128)(2,1)} async-done(((bf16[256,3584]{1,0:T(8,128)(2,1)}), bf16[64,3584]{1,0:T(8,128)(2,1)}) %reduce-scatter.2.cloned.1.call-update) | async-done | bytes 458768 | tf_op jit(solution)/shard_map/reduce_scatter | solution.py:115
  74.5 1.2 fusion.8
  75.7 0.0 copy-done.2
  75.7 0.0 copy-done.3
  75.7 1.4 fusion.12
  77.1 0.0 copy-start.1
  77.2 0.0 copy-done.4
  77.2 0.9 fusion.14
  78.1 0.0 all-gather.6.cloned.1.call-update
  78.1 0.0 all-gather.8.cloned.1.call-start
  78.2 0.7 all-gather.8.cloned.1.call-update
  78.9 0.0 all-gather.10.cloned.1.call-start
  78.9 0.5 all-gather.10.cloned.1.call-update
  79.5 0.0 copy-done.1
  79.5 39.2 %all-gather.6.cloned.1.call-done = bf16[256,3584]{1,0:T(8,128)(2,1)} async-done(((bf16[64,3584]{1,0:T(8,128)(2,1)}), bf16[256,3584]{1,0:T(8,128)(2,1)}) %all-gather.6.cloned.1.call-update) | async-done | bytes 1835024 | tf_op jit(solution)/shard_map/all_gather | solution.py:125
  118.7 47.5 %all-gather.8.cloned.1.call-done = bf16[3584,896]{1,0:T(8,128)(2,1)} async-done(((bf16[896,896]{1,0:T(8,128)(2,1)}), bf16[3584,896]{1,0:T(8,128)(2,1)}) %all-gather.8.cloned.1.call-update) | async-done | bytes 6422544 | tf_op jit(solution)/shard_map/all_gather | solution.py:127
  166.2 5.5 %fusion.52 = f32[256,896]{1,0:T(8,128)S(1)} fusion(bf16[256,3584]{1,0:T(8,128)(2,1)} %all-gather.6.cloned.1.call-done, bf16[3584,896]{1,0:T(8,128)(2,1)} %all-gather.8.cloned.1.call-done), kind=kOutput, calls=%fused_computation.83 | convolution fusion | flops 1644167168 | bytes 9175040 | tf_op jit(solution)/shard_map/dot_general | solution.py:130
  171.6 43.1 %all-gather.10.cloned.1.call-done = bf16[3584,896]{1,0:T(8,128)(2,1)} async-done(((bf16[896,896]{1,0:T(8,128)(2,1)}), bf16[3584,896]{1,0:T(8,128)(2,1)}) %all-gather.10.cloned.1.call-update) | async-done | bytes 6422544 | tf_op jit(solution)/shard_map/all_gather | solution.py:128
  214.7 6.3 %fusion.5 = bf16[256,896]{1,0:T(8,128)(2,1)} fusion(bf16[256,3584]{1,0:T(8,128)(2,1)} %all-gather.6.cloned.1.call-done, bf16[3584,896]{1,0:T(8,128)(2,1)} %all-gather.10.cloned.1.call-done, f32[256,896]{1,0:T(8,128)S(1)} %fusion.52), kind=kOutput, calls=%fused_computation.9 | convolution fusion | flops 1646460928 | bytes 9633792 | tf_op jit(solution)/shard_map/dot_general | solution.py:131
  (8 shorter events, 0.1 us)
Async XLA Ops:
  7.2 24.7 %copy-start = (bf16[256,3584]{1,0:T(8,128)(2,1)S(1)}, bf16[256,3584]{1,0:T(8,128)(2,1)}, u32[]{:S(2)}) copy-start(bf16[256,3584]{1,0:T(8,128)(2,1)} %param.15) | copy-start | bytes 5505028
  7.2 67.3 %reduce-scatter.2.cloned.1.call-start = ((), (), s32[]{:S(2)}) async-start(), calls=%async_computation.1 | async-start | bytes 2293760 | tf_op jit(solution)/shard_map/reduce_scatter | solution.py:115
  8.2 6.6 %collective-permute-start = (bf16[2,256,128]{2,1,0:T(8,128)(2,1)S(1)}, bf16[2,256,128]{2,1,0:T(8,128)(2,1)S(1)}, u32[]{:S(2)}, u32[]{:S(2)}) collective-permute-start(bf16[2,256,128]{2,1,0:T(8,128)(2,1)S(1)} %pad_maximum_fusion), channel_id=1, source_target_pairs={{0,1},{1,0},{2,3},{3,2},{4,5},{5,4},{6,7},{7,6},{8,9},{9,8},{10,11... | collective-permute-start | bytes 393224 | tf_op jit(solution)/shard_map/ppermute | solution.py:15
  34.2 41.5 %copy-start.2 = (bf16[64,3584]{1,0:T(8,128)(2,1)S(1)}, bf16[64,3584]{1,0:T(8,128)(2,1)}, u32[]{:S(2)}) copy-start(bf16[64,3584]{1,0:T(8,128)(2,1)} %param.10) | copy-start | bytes 1376260
  34.2 41.5 %copy-start.3 = (f32[3584]{0:T(1024)S(1)}, f32[3584]{0:T(1024)}, u32[]{:S(2)}) copy-start(f32[3584]{0:T(1024)} %param.16) | copy-start | bytes 43012
  34.2 43.0 %copy-start.4 = (f32[3584]{0:T(1024)S(1)}, f32[3584]{0:T(1024)}, u32[]{:S(2)}) copy-start(f32[3584]{0:T(1024)} %param.17) | copy-start | bytes 43012
  34.2 84.4 %all-gather.6.cloned.1.call-start = ((), (), s32[]{:S(2)}) async-start(), calls=%async_computation.2 | async-start | bytes 2293760 | tf_op jit(solution)/shard_map/all_gather | solution.py:125
  77.1 2.3 %copy-start.1 = (bf16[64,3584]{1,0:T(8,128)(2,1)}, bf16[64,3584]{1,0:T(8,128)(2,1)S(1)}, u32[]{:S(2)}) copy-start(bf16[64,3584]{1,0:T(8,128)(2,1)S(1)} %get-tuple-element.3) | copy-start | bytes 1376260
  78.1 88.0 %all-gather.8.cloned.1.call-start = ((), (), s32[]{:S(2)}) async-start(), calls=%async_computation.3 | async-start | bytes 8028160 | tf_op jit(solution)/shard_map/all_gather | solution.py:127
  78.9 135.9 %all-gather.10.cloned.1.call-start = ((), (), s32[]{:S(2)}) async-start(), calls=%async_computation.4 | async-start | bytes 8028160 | tf_op jit(solution)/shard_map/all_gather | solution.py:128
Sparse Core Ops, SparseCore 0:
  34.4 40.0 reduce-scatter.1
  78.3 40.3 all-gather.5
  120.2 45.9 all-gather.7
  167.6 47.0 all-gather.9
where the time goes:
time: 228 us
  waiting for transfers between devices  173 us (76%)
  matrix products  14.8 us (6%)
  blocking collectives  14.6 us (6%)
  between operations  13.9 us (6%)
  other arithmetic  8.2 us (4%)
  starting transfers between devices  3.28 us (1%)
    all_gather x1, waiting for transfers between devices, per_device(): lax.all_gather(gate_weight, 'ctx', axis=0, tiled=True)  47.5 us
    all_gather x1, waiting for transfers between devices, per_device(): lax.all_gather(up_weight, 'ctx', axis=0, tiled=True)  43.1 us
    reduce_scatter x1, waiting for transfers between devices, per_device(): lax.psum_scatter(jnp.dot(attended, out_weight, preferred_element_type=jnp...  40.2 us
    all_gather x1, waiting for transfers between devices, per_device(): gathered_rows = lax.all_gather(ffn_input, 'tensor', axis=0, tiled=True)  39.2 us
    all_gather x1, blocking collectives, per_device(): lax.all_gather(key_rot, 'ctx', axis=0, tiled=True)  7.34 us
    all_gather x1, blocking collectives, per_device(): lax.all_gather(joined[1], 'ctx', axis=0, tiled=True)  7.26 us
    dot_general x1, matrix products, per_device(): jnp.dot(gathered_rows, shard_pair[1], preferred_element_type=jnp.float32)  6.25 us
    dot_general x1, matrix products, per_device(): jnp.dot(gathered_rows, shard_pair[0], preferred_element_type=jnp.float32)  5.45 us
  transfers between devices with their start and end apart: 5, of which 5 were waited for; matrix products, arithmetic and copies ran while one was open for 3% of the time, Pallas kernels for 0%

commit v1 on v0

--- a/solution.py
+++ b/solution.py
@@ -122,7 +122,10 @@
         jnp.bfloat16
     )
     ffn_input = (rms_scale(mixed_stream.astype(jnp.float32)) * ffn_gain).astype(jnp.bfloat16)
-    gathered_rows = lax.all_gather(ffn_input, "tensor", axis=0, tiled=True)
+    d_next = lax.axis_size("tensor")
+    opened = jnp.stack(d_next * [ffn_input])
+    local_now = lax.all_to_all(opened, axis_name="tensor", split_axis=0, concat_axis=0)
+    gathered_rows = jnp.concatenate(local_now, axis=0)
     shard_pair = (
         lax.all_gather(gate_weight, "ctx", axis=0, tiled=True),
         lax.all_gather(up_weight, "ctx", axis=0, tiled=True),

time: 228 us -> 147 us (0.64)
  waiting for transfers between devices: 173 us -> 45.3 us
  blocking collectives: 14.6 us -> 60.3 us
    all_gather x1, waiting for transfers between devices: 47.5 us -> 0.01 us  [per_device(): lax.all_gather(gate_weight, 'ctx', axis=0, tiled=True)]
    all_to_all x0 -> x1, blocking collectives: none -> 45.7 us  [per_device(): lax.all_to_all(opened, axis_name='tensor', split_axis=0, concat_axis=0)]
    all_gather x1, waiting for transfers between devices: 43.1 us -> 3.64 us  [per_device(): lax.all_gather(up_weight, 'ctx', axis=0, tiled=True)]
    all_gather x1 -> x0, waiting for transfers between devices: 39.2 us -> none  [per_device(): gathered_rows = lax.all_gather(ffn_input, 'tensor', axis=0, tiled=True)]
  transfers between devices with their start and end apart: 5 -> 4, of which waited for: 5 -> 3; matrix products, arithmetic and copies ran while one was open for 3% -> 7% of each run, Pallas kernels for 0% -> 0%
where the time goes in v1:
time: 147 us
  blocking collectives  60.3 us (41%)
  waiting for transfers between devices  45.3 us (31%)
  between operations  15.6 us (11%)
  matrix products  14.8 us (10%)
  other arithmetic  7.47 us (5%)
  starting transfers between devices  3.24 us (2%)
    all_to_all x1, blocking collectives, per_device(): lax.all_to_all(opened, axis_name='tensor', split_axis=0, concat_axis=0)  45.7 us
    reduce_scatter x1, waiting for transfers between devices, per_device(): lax.psum_scatter(jnp.dot(attended, out_weight, preferred_element_type=jnp...  39 us
    all_gather x1, blocking collectives, per_device(): lax.all_gather(key_rot, 'ctx', axis=0, tiled=True)  7.34 us
    all_gather x1, blocking collectives, per_device(): lax.all_gather(joined[1], 'ctx', axis=0, tiled=True)  7.26 us
    dot_general x1, matrix products, per_device(): jnp.dot(gathered_rows, shard_pair[1], preferred_element_type=jnp.float32)  6.25 us
    dot_general x1, matrix products, per_device(): jnp.dot(gathered_rows, shard_pair[0], preferred_element_type=jnp.float32)  5.45 us
    all_gather x1, waiting for transfers between devices, per_device(): lax.all_gather(up_weight, 'ctx', axis=0, tiled=True)  3.64 us
    ppermute x1, starting transfers between devices, partner_2(): return lax.ppermute(value, axis, pairs)  3.12 us
  transfers between devices with their start and end apart: 4, of which 3 were waited for; matrix products, arithmetic and copies ran while one was open for 7% of the time, Pallas kernels for 0%

profile of v1, /device:TPU:0, one launch (start us, length us, event | category | flops | bytes accessed | tf_op | source)
XLA Modules:
  0.0 146.8 jit_solution(14910882615770059241)
XLA Ops:
  8.0 0.0 copy-start
  8.0 0.0 reduce-scatter.2.cloned.1.call-start
  8.1 1.0 pad_maximum_fusion
  9.1 3.1 %collective-permute-start = (bf16[2,256,128]{2,1,0:T(8,128)(2,1)S(1)}, bf16[2,256,128]{2,1,0:T(8,128)(2,1)S(1)}, u32[]{:S(2)}, u32[]{:S(2)}) collective-permute-start(bf16[2,256,128]{2,1,0:T(8,128)(2,1)S(1)} %pad_maximum_fusion), channel_id=1, source_target_pairs={{0,1},{1,0},{2,3},{3,2},{4,5},{5,4},{6,7},{7,6},{8,9},{9,8},{10,11... | collective-permute-start | bytes 393224 | tf_op jit(solution)/shard_map/ppermute | solution.py:15
  12.2 0.9 bitcast_convert_fusion
  13.1 0.8 reduce-window.8
  14.0 0.1 convert_reduce_fusion.2
  14.1 0.1 convert_reduce_fusion.1
  14.2 1.5 %collective-permute-done = bf16[2,256,128]{2,1,0:T(8,128)(2,1)S(1)} collective-permute-done((bf16[2,256,128]{2,1,0:T(8,128)(2,1)S(1)}, bf16[2,256,128]{2,1,0:T(8,128)(2,1)S(1)}, u32[]{:S(2)}, u32[]{:S(2)}) %collective-permute-start) | collective-permute-done | bytes 131104 | tf_op jit(solution)/shard_map/ppermute | solution.py:15
  15.7 1.0 maximum_select_fusion
  16.7 0.6 fusion.34
  17.4 7.3 %all-gather = bf16[1024,1,256]{2,0,1:T(8,128)(2,1)S(1)} all-gather(bf16[256,1,256]{2,0,1:T(8,128)(2,1)S(1)} %pad_maximum_fusion.1), channel_id=2, replica_groups=mesh['dp'=2,'ctx'=4,'tensor'=4] {'ctx'}, dimensions={0}, use_global_device_ids=true | all-gather | bytes 655360 | tf_op jit(solution)/shard_map/all_gather | solution.py:100
  24.7 7.3 %all-gather.1 = bf16[1,1024,256]{2,1,0:T(8,128)(2,1)S(1)} all-gather(bf16[1,256,256]{2,1,0:T(8,128)(2,1)S(1)} %get-tuple-element.8), channel_id=3, replica_groups=mesh['dp'=2,'ctx'=4,'tensor'=4] {'ctx'}, dimensions={1}, use_global_device_ids=true | all-gather | bytes 655360 | tf_op jit(solution)/shard_map/all_gather | solution.py:101
  32.0 0.7 convert_reduce_fusion
  32.7 0.0 copy-done
  32.7 2.4 %convolution_convert_fusion = bf16[256,3584]{1,0:T(8,128)(2,1)} fusion(bf16[256,3584]{1,0:T(8,128)(2,1)S(1)} %copy-done, bf16[256,1024]{1,0:T(8,128)(2,1)S(1)} %get-tuple-element.13, bf16[1,1024,256]{2,1,0:T(8,128)(2,1)S(1)} %all-gather.1, f32[256]{0:T(256)S(1)} %get-tuple-element.12), kind=kOutput, calls=%fused_computation | convolution fusion | flops 605028352 | bytes 4719616 | tf_op jit(solution)/shard_map/dot_general | solution.py:116
  35.1 0.0 reduce-scatter.2.cloned.1.call-update
  35.1 0.0 copy-start.2
  35.1 0.0 copy-start.3
  35.1 0.0 all-gather.5.cloned.1.call-start
  35.2 0.5 all-gather.5.cloned.1.call-update
  35.7 0.0 copy-start.4
  35.7 0.0 all-gather.7.cloned.1.call-start
  35.7 0.5 all-gather.7.cloned.1.call-update
  36.3 39.0 %reduce-scatter.2.cloned.1.call-done = bf16[64,3584]{1,0:T(8,128)(2,1)} async-done(((bf16[256,3584]{1,0:T(8,128)(2,1)}), bf16[64,3584]{1,0:T(8,128)(2,1)}) %reduce-scatter.2.cloned.1.call-update) | async-done | bytes 458768 | tf_op jit(solution)/shard_map/reduce_scatter | solution.py:115
  75.3 1.2 fusion.8
  76.6 0.0 copy-done.2
  76.6 0.0 copy-done.3
  76.6 1.4 fusion.12
  78.0 0.0 copy-start.1
  78.0 0.0 copy-done.4
  78.1 0.2 fusion.14
  78.2 0.1 stack.19
  78.4 45.7 %all_to_all.5 = bf16[4,64,3584]{2,1,0:T(8,128)(2,1)} all-to-all(bf16[4,64,3584]{2,1,0:T(8,128)(2,1)S(1)} %stack.19), channel_id=1, replica_groups=mesh['dp'=2,'ctx'=4,'tensor'=4] {'tensor'}, dimensions={0} | all-to-all | bytes 3670016 | tf_op jit(solution)/shard_map/all_to_all | solution.py:127
  124.0 0.0 copy-done.1
  124.0 0.0 all-gather.5.cloned.1.call-done
  124.0 5.4 %fusion.52 = f32[256,896]{1,0:T(8,128)S(1)} fusion(bf16[256,3584]{1,0:T(8,128)(2,1)} %bitcast.33, bf16[3584,896]{1,0:T(8,128)(2,1)} %all-gather.5.cloned.1.call-done), kind=kOutput, calls=%fused_computation.83 | convolution fusion | flops 1644167168 | bytes 9175040 | tf_op jit(solution)/shard_map/dot_general | solution.py:133
  129.5 3.6 %all-gather.7.cloned.1.call-done = bf16[3584,896]{1,0:T(8,128)(2,1)} async-done(((bf16[896,896]{1,0:T(8,128)(2,1)}), bf16[3584,896]{1,0:T(8,128)(2,1)}) %all-gather.7.cloned.1.call-update) | async-done | bytes 6422544 | tf_op jit(solution)/shard_map/all_gather | solution.py:131
  133.1 6.3 %fusion.5 = bf16[256,896]{1,0:T(8,128)(2,1)} fusion(bf16[256,3584]{1,0:T(8,128)(2,1)} %bitcast.34, bf16[3584,896]{1,0:T(8,128)(2,1)} %all-gather.7.cloned.1.call-done, f32[256,896]{1,0:T(8,128)S(1)} %fusion.52), kind=kOutput, calls=%fused_computation.9 | convolution fusion | flops 1646460928 | bytes 9633792 | tf_op jit(solution)/shard_map/dot_general | solution.py:134
  (8 shorter events, 0.1 us)
Async XLA Ops:
  8.0 24.7 %copy-start = (bf16[256,3584]{1,0:T(8,128)(2,1)S(1)}, bf16[256,3584]{1,0:T(8,128)(2,1)}, u32[]{:S(2)}) copy-start(bf16[256,3584]{1,0:T(8,128)(2,1)} %param.15) | copy-start | bytes 5505028
  8.0 67.3 %reduce-scatter.2.cloned.1.call-start = ((), (), s32[]{:S(2)}) async-start(), calls=%async_computation.2 | async-start | bytes 2293760 | tf_op jit(solution)/shard_map/reduce_scatter | solution.py:115
  9.1 6.6 %collective-permute-start = (bf16[2,256,128]{2,1,0:T(8,128)(2,1)S(1)}, bf16[2,256,128]{2,1,0:T(8,128)(2,1)S(1)}, u32[]{:S(2)}, u32[]{:S(2)}) collective-permute-start(bf16[2,256,128]{2,1,0:T(8,128)(2,1)S(1)} %pad_maximum_fusion), channel_id=1, source_target_pairs={{0,1},{1,0},{2,3},{3,2},{4,5},{5,4},{6,7},{7,6},{8,9},{9,8},{10,11... | collective-permute-start | bytes 393224 | tf_op jit(solution)/shard_map/ppermute | solution.py:15
  35.1 41.5 %copy-start.2 = (bf16[64,3584]{1,0:T(8,128)(2,1)S(1)}, bf16[64,3584]{1,0:T(8,128)(2,1)}, u32[]{:S(2)}) copy-start(bf16[64,3584]{1,0:T(8,128)(2,1)} %param.10) | copy-start | bytes 1376260
  35.1 41.5 %copy-start.3 = (f32[3584]{0:T(1024)S(1)}, f32[3584]{0:T(1024)}, u32[]{:S(2)}) copy-start(f32[3584]{0:T(1024)} %param.16) | copy-start | bytes 43012
  35.1 88.9 %all-gather.5.cloned.1.call-start = ((), (), s32[]{:S(2)}) async-start(), calls=%async_computation.3 | async-start | bytes 8028160 | tf_op jit(solution)/shard_map/all_gather | solution.py:130
  35.7 42.4 %copy-start.4 = (f32[3584]{0:T(1024)S(1)}, f32[3584]{0:T(1024)}, u32[]{:S(2)}) copy-start(f32[3584]{0:T(1024)} %param.17) | copy-start | bytes 43012
  35.7 97.4 %all-gather.7.cloned.1.call-start = ((), (), s32[]{:S(2)}) async-start(), calls=%async_computation.4 | async-start | bytes 8028160 | tf_op jit(solution)/shard_map/all_gather | solution.py:131
  78.0 46.0 %copy-start.1 = (bf16[64,3584]{1,0:T(8,128)(2,1)}, bf16[64,3584]{1,0:T(8,128)(2,1)S(1)}, u32[]{:S(2)}) copy-start(bf16[64,3584]{1,0:T(8,128)(2,1)S(1)} %get-tuple-element.3) | copy-start | bytes 1376260
Sparse Core Ops, SparseCore 0:
  35.2 40.0 reduce-scatter.1
Sparse Core Ops, SparseCore 1:
  37.1 47.5 all-gather.4
  86.1 46.9 all-gather.6
